TPU v7x, 32 devices: a whole 2x2x4 slice. The times are simulated.
32 devices in a mesh: col: 8 (over z, y), row: 4 (over x, core).
Axes of the slice: x: 2, y: 2, z: 4, core: 2. Of those that a mesh axis runs over, the one named last changes fastest.
Arguments:
- sigma_anc: float32 [16, 16, 128, 128], P('row', 'col'), as said below
- panel_u: float32 [8, 8, 128, 128], P('col'), may hold values from -0.1875 to 0.1875
- structure: int32 [8, 8], P('col'), may hold values from 0 to 15, as said below
- diag_inv: float32 [8, 128, 128], P('col'), may hold values from -0.5 to 0.5
Outputs:
- panel_out: float32 [8, 16, 128, 128], P('col', 'row')
- diag_out: float32 [8, 128, 128], P('col')
Inputs may be any that keep to these rules, and one draw needn't show every extreme that they name: `structure`: each row holds 8 different ancestor numbers in increasing order. `sigma_anc`: the matrix is symmetric: block (a, b) is the transpose of block (b, a).
All inputs are finite; a program needn't handle non-finite values.
Results may differ from a plain program's by a relative error of at most 0.0003.
Values sent between devices are 32-bit elements; how exact they have to be, the bound alone decides.
A program may use at most 128 MiB of HBM per device.

v0:
```python
import jax
import jax.numpy as jnp
from jax import lax
from jax.sharding import PartitionSpec as P


def local(sigma_anc, panel_u, structure, diag_inv):
    row_count = sigma_anc.shape[0]
    col_count = sigma_anc.shape[1]
    total_anc = col_count * lax.axis_size("col")
    ancestors = jnp.arange(total_anc, dtype=jnp.int32)
    onehot = (structure[:, :, None] == ancestors[None, None, :]).astype(jnp.float32)
    row_start = lax.axis_index("row") * row_count
    dense = jnp.einsum("jka,jkxy->ajxy", onehot, panel_u, precision=lax.Precision.HIGHEST)
    local_rows = lax.dynamic_slice_in_dim(dense, row_start, row_count, 0)
    moved = lax.all_to_all(dense, "col", split_axis=0, concat_axis=1, tiled=True)
    summed = lax.psum_scatter(
        jnp.einsum("abxz,bjzy->jaxy", sigma_anc, moved, precision=lax.Precision.HIGHEST),
        "col",
        scatter_dimension=0,
        tiled=True,
    )
    local_anc = row_start + jnp.arange(row_count, dtype=jnp.int32)
    member = jnp.any(structure[:, :, None] == local_anc[None, None, :], axis=1).astype(jnp.float32)
    panel_out = -summed * member[:, :, None, None]
    share = jnp.einsum("ajzx,jazy->jxy", local_rows, panel_out, precision=lax.Precision.HIGHEST)
    update = lax.psum(share, "row")
    base = jnp.einsum("jzx,jzy->jxy", diag_inv, diag_inv, precision=lax.Precision.HIGHEST)
    return (panel_out, base - update)


def solution(mesh):
    placed = (
        P("row", "col", None, None),
        P("col", None, None, None),
        P("col", None),
        P("col", None, None),
    )
    return jax.shard_map(
        local,
        mesh=mesh,
        in_specs=placed,
        out_specs=(P("col", "row", None, None), P("col", None, None)),
        check_vma=False,
    )
```

profile of v0, /device:TPU:1, one launch (start us, length us, event | category | flops | bytes accessed | tf_op | source)
XLA Modules:
  0.0 154.7 jit_solution(1103796969047341646)
XLA Ops:
  7.2 0.0 copy-start
  7.2 0.0 reduce-scatter.2.cloned.1.call-start
  7.2 2.0 %fusion.2 = f32[16,128,128]{2,0,1:T(8,128)S(1)} fusion(f32[8,128,128]{2,1,0:T(8,128)} %bitcast.45, s32[8]{0:T(128)} %bitcast.46), kind=kOutput, calls=%fused_computation.5 | convolution fusion | flops 25165952 | bytes 1572896 | tf_op jit(solution)/shard_map/jka,jkxy->ajxy/dot_general | solution.py:14
  9.2 0.3 copy.18
  9.5 31.1 %all_to_all.18 = f32[16,1,128,128]{3,2,1,0:T(8,128)} all-to-all(f32[16,1,128,128]{3,2,1,0:T(8,128)S(1)} %copy.18), channel_id=1, replica_groups=mesh['col'=8,'row'=4] {'col'}, dimensions={0} | all-to-all | bytes 2097152 | tf_op jit(solution)/shard_map/all_to_all | solution.py:16
  40.7 1.6 %copy.19 = f32[16,1,128,128]{2,3,0,1:T(8,128)S(1)} copy(f32[16,1,128,128]{3,2,1,0:T(8,128)} %all_to_all.18) | data formatting | bytes 2097152 | tf_op jit(solution)/shard_map/all_to_all | solution.py:16
  42.2 0.0 copy-done
  42.3 0.0 copy-start.2
  42.3 3.2 %convolution_bitcast_fusion = f32[8,4,128,128]{2,3,1,0:T(8,128)} fusion(f32[2,8,128,128,1]{2,3,0,4,1:T(8,128)S(1)} %bitcast.44, f32[4,2,128,128]{3,2,1,0:T(8,128)S(1)} %copy-done), kind=kOutput, calls=%fused_computation | convolution fusion | flops 1610612736 | bytes 3670016 | tf_op jit(solution)/shard_map/abxz,bjzy->jaxy/dot_general | solution.py:18
  45.5 0.0 copy-start.1
  45.5 0.0 reduce-scatter.2.cloned.1.call-update
  45.5 0.0 all-reduce.2.cloned.1.call-start
  45.6 0.0 copy-done.2
  45.6 0.2 compare_reduce_fusion
  45.8 0.1 constant_dynamic-slice_fusion
  45.8 66.9 %reduce-scatter.2.cloned.1.call-done = f32[1,4,128,128]{2,3,1,0:T(8,128)} async-done(((f32[8,4,128,128]{2,3,1,0:T(8,128)}), f32[1,4,128,128]{2,3,1,0:T(8,128)}) %reduce-scatter.2.cloned.1.call-update) | async-done | bytes 262160 | tf_op jit(solution)/shard_map/reduce_scatter | solution.py:17
  112.7 1.0 negate_multiply_fusion
  113.7 1.2 convolution_bitcast_fusion.2
  115.0 0.0 all-reduce.2.cloned.1.call-update
  115.0 0.8 copy.22
  115.8 30.3 %all-reduce.2.cloned.1.call-done = f32[1,128,128]{2,1,0:T(8,128)} async-done(((f32[1,128,128]{2,1,0:T(8,128)}), f32[1,128,128]{2,1,0:T(8,128)}) %all-reduce.2.cloned.1.call-update) | async-done | bytes 65552 | tf_op jit(solution)/shard_map/psum | solution.py:27
  146.1 0.0 copy-done.1
  146.1 1.8 %fusion = f32[1,128,128]{2,1,0:T(8,128)} fusion(f32[1,128,128]{2,1,0:T(8,128)} %all-reduce.2.cloned.1.call-done, f32[1,128,128]{2,1,0:T(8,128)S(1)} %copy-done.1), kind=kOutput, calls=%fused_computation.3 | convolution fusion | flops 25182208 | bytes 196608 | tf_op jit(solution)/shard_map/jzx,jzy->jxy/dot_general | solution.py:28
  (2 shorter events, 0.0 us)
Async XLA Ops:
  7.2 35.1 %copy-start = (f32[4,2,128,128]{3,2,1,0:T(8,128)S(1)}, f32[4,2,128,128]{3,2,1,0:T(8,128)}, u32[]{:S(2)}) copy-start(f32[4,2,128,128]{3,2,1,0:T(8,128)} %param.4) | copy-start | bytes 1572868
  7.2 105.5 %reduce-scatter.2.cloned.1.call-start = ((), (), s32[]{:S(2)}) async-start(), calls=%async_computation.2 | async-start | bytes 2359296 | tf_op jit(solution)/shard_map/reduce_scatter | solution.py:17
  42.3 3.3 %copy-start.2 = (s32[1,8]{1,0:T(1,128)S(1)}, s32[1,8]{1,0:T(1,128)}, u32[]{:S(2)}) copy-start(s32[1,8]{1,0:T(1,128)} %param.6) | copy-start | bytes 100
  45.5 100.6 %copy-start.1 = (f32[1,128,128]{2,1,0:T(8,128)S(1)}, f32[1,128,128]{2,1,0:T(8,128)}, u32[]{:S(2)}) copy-start(f32[1,128,128]{2,1,0:T(8,128)} %param.7) | copy-start | bytes 196612
  45.5 100.6 %all-reduce.2.cloned.1.call-start = ((), (), s32[]{:S(2)}) async-start(), calls=%async_computation.3 | async-start | bytes 131072 | tf_op jit(solution)/shard_map/psum | solution.py:27
Sparse Core Ops, SparseCore 0:
  45.6 67.0 reduce-scatter.1
  115.6 30.4 all-reduce.1
where the time goes:
time: 157 us; the launch traced here: 155 us
  waiting for transfers between devices  97.2 us (62%)
  blocking collectives  31.1 us (20%)
  between operations  14.1 us (9%)
  matrix products  8.14 us (5%)
  local copies, waits for them, and re-layouts  2.8 us (2%)
    reduce_scatter x1, waiting for transfers between devices, local(): lax.psum_scatter(jnp.einsum('abxz,bjzy->jaxy', sigma_anc, moved, precisio...  66.9 us
    all_to_all x1, blocking collectives, local(): lax.all_to_all(dense, 'col', split_axis=0, concat_axis=1, tiled=True)  31.1 us
    psum x1, waiting for transfers between devices, local(): update = lax.psum(share, 'row')  30.3 us
    dot_general x1, matrix products, local(): jnp.einsum('abxz,bjzy->jaxy', sigma_anc, moved, precision=lax.Precision.H...  3.2 us
  transfers between devices with their start and end apart: 2, of which 2 were waited for; matrix products, arithmetic and copies ran while one was open for 1% of the time, Pallas kernels for 0%

commit v1 on v0

v1 whole, which is shorter than its diff:
```python
import functools

import jax
import jax.numpy as jnp
from jax import lax
from jax.experimental import pallas as pl
from jax.experimental.pallas import tpu as pltpu
from jax.sharding import PartitionSpec as P

MESH = pl.DeviceIdType.MESH
HIGHEST = lax.Precision.HIGHEST


def split(x):
    high = x.astype(jnp.bfloat16)
    return high, (x - high.astype(jnp.float32)).astype(jnp.bfloat16)


def dot_t(a, b):
    return lax.dot_general(
        a, b, (((0,), (0,)), ((), ())), precision=HIGHEST, preferred_element_type=jnp.float32
    )


def kernel(
    planes,
    rows,
    chunks,
    sigma_ref,
    u_ref,
    s_ref,
    inv_ref,
    panel_ref,
    diag_ref,
    dense,
    moved,
    other,
    sig_hi,
    sig_lo,
    w_cat,
    sums,
    came,
    share,
    shares,
    y_send,
    y_recv,
    w_send,
    w_recv,
    f_send,
    f_recv,
    r_send,
    r_recv,
    d_send,
    d_recv,
):
    row_count, col_count, width = sigma_ref.shape[0], sigma_ref.shape[1], sigma_ref.shape[2]
    plane_cols = 2 * col_count
    step_rows = row_count // chunks
    col, row = lax.axis_index("col"), lax.axis_index("row")
    z, y = col // 2, col % 2
    half = row % 2
    mate = row + 1 - 2 * half
    entries = u_ref.shape[1]

    def at(plane, lane=None, line=None):
        lane = y if lane is None else lane
        return {"col": plane * 2 + lane, "row": row if line is None else line}

    def order(n):
        right_first = jnp.where(n < planes - 1 - z, planes - 1 - n, n - (planes - 1 - z))
        left_first = jnp.where(n < z, n, planes - 1 - (n - z))
        return jnp.where(2 * z < planes, right_first, left_first)

    barrier = pltpu.get_barrier_semaphore()
    pl.semaphore_signal(barrier, inc=1, device_id=at(z, 1 - y), device_id_type=MESH)

    @pl.loop(0, planes - 1)
    def _(n):
        pl.semaphore_signal(barrier, inc=1, device_id=at(order(n)), device_id_type=MESH)

    for o in range(1, rows):
        pl.semaphore_signal(
            barrier, inc=1, device_id=at(z, None, lax.rem(row + o, rows)), device_id_type=MESH
        )

    def member(b):
        found, where = jnp.int32(0), jnp.int32(0)
        for k in range(entries):
            hit = s_ref[0, k] == b
            found, where = jnp.where(hit, 1, found), jnp.where(hit, k, where)
        return found.astype(jnp.float32), where

    @pl.loop(0, dense.shape[0])
    def _(b):
        found, where = member(b)
        dense[b] = u_ref[0, where] * found

    inv = inv_ref[0]
    diag_ref[0] = dot_t(inv, inv)

    def plane_part(plane, part):
        lane = jnp.where(part == 0, y, 1 - y)
        return plane * plane_cols + lane * col_count

    for part in range(2):
        for i in range(col_count):
            moved[z, part * col_count + i] = dense[plane_part(z, part) + i]

    pl.semaphore_wait(barrier, planes - 1 + 1 + rows - 1)

    def y_copy(c):
        rng = pl.ds(c * step_rows, step_rows)
        return pltpu.make_async_remote_copy(
            sigma_ref.at[rng], other.at[rng], y_send.at[c], y_recv.at[c], at(z, 1 - y), MESH
        )

    def w_copy(target):
        return pltpu.make_async_remote_copy(
            dense.at[pl.ds(plane_part(target, half), col_count)],
            moved.at[z, pl.ds(half * col_count, col_count)],
            w_send.at[target],
            w_recv.at[z],
            at(target),
            MESH,
        )

    def w_arrival(source):
        mine = moved.at[source, pl.ds(half * col_count, col_count)]
        return pltpu.make_async_remote_copy(
            mine, mine, w_send.at[source], w_recv.at[source], at(source), MESH
        )

    def f_copy(source):
        mine = moved.at[source, pl.ds(half * col_count, col_count)]
        return pltpu.make_async_remote_copy(
            mine, mine, f_send.at[source], f_recv.at[source], at(z, None, mate), MESH
        )

    def f_arrival(source):
        theirs = moved.at[source, pl.ds((1 - half) * col_count, col_count)]
        return pltpu.make_async_remote_copy(
            theirs, theirs, f_send.at[source], f_recv.at[source], at(z, None, mate), MESH
        )

    def r_copy(d, c, slot, target):
        rng = pl.ds(c * step_rows, step_rows)
        return pltpu.make_async_remote_copy(
            sums.at[d, rng], came.at[slot, rng], r_send.at[d, c], r_recv.at[slot, c], at(target), MESH
        )

    def r_arrival(slot, c):
        rng = pl.ds(c * step_rows, step_rows)
        return pltpu.make_async_remote_copy(
            came.at[slot, rng], came.at[slot, rng], r_send.at[0, c], r_recv.at[slot, c], at(z, 1 - y), MESH
        )

    for c in range(chunks):
        y_copy(c).start()

    @pl.loop(0, planes - 1)
    def _(n):
        w_copy(order(n)).start()

    def forward(source):
        w_arrival(source).wait_recv()
        f_copy(source).start()

    def load_w(d):
        for i in range(plane_cols):
            high, low = split(moved[d, i])
            w_cat[i * width : (i + 1) * width, :width] = high
            w_cat[i * width : (i + 1) * width, width:] = low

    def convert(c):
        for q in range(step_rows):
            a = c * step_rows + q
            for source, base in ((sigma_ref, 0), (other, col_count)):
                for i in range(col_count):
                    high, low = split(source[a, i])
                    lanes = slice((base + i) * width, (base + i + 1) * width)
                    sig_hi[a, :, lanes] = high
                    sig_lo[a, :, lanes] = low

    def product(a):
        both = jnp.dot(sig_hi[a], w_cat[...], preferred_element_type=jnp.float32)
        low = jnp.dot(sig_lo[a], w_cat[:, :width], preferred_element_type=jnp.float32)
        return both[:, :width] + (both[:, width:] + low)

    forward(order(0))

    @pl.loop(0, planes - 1)
    def _(n):
        d = order(n)
        right = d > z
        f_arrival(d).wait_recv()
        load_w(d)
        has_up = jnp.where(right, z > 0, z < planes - 1)
        target = jnp.where(right, z + 1, z - 1)
        slot = jnp.where(right, d, jnp.where(d == z - 1, planes, d))
        for c in range(chunks):

            @pl.when(n == 0)
            def _():
                y_copy(c).wait_recv()
                convert(c)

            for q in range(step_rows):
                a = c * step_rows + q
                sums[d, a] = product(a)

            @pl.when(has_up)
            def _():
                r_arrival(d, c).wait_recv()
                for q in range(step_rows):
                    a = c * step_rows + q
                    sums[d, a] += came[d, a]

            r_copy(d, c, slot, target).start()

            if c == chunks // 2:

                @pl.when(n + 1 < planes - 1)
                def _():
                    forward(order(n + 1))

    load_w(z)
    for a in range(row_count):
        sums[z, a] = product(a)
    row_start = row * row_count
    total = jnp.zeros((width, width), jnp.float32)
    for c in range(chunks):

        @pl.when(z > 0)
        def _():
            r_arrival(z, c).wait_recv()
            for q in range(step_rows):
                a = c * step_rows + q
                sums[z, a] += came[z, a]

        @pl.when(z < planes - 1)
        def _():
            r_arrival(planes, c).wait_recv()
            for q in range(step_rows):
                a = c * step_rows + q
                sums[z, a] += came[planes, a]

        for q in range(step_rows):
            a = c * step_rows + q
            found, _ = member(row_start + a)
            panel = -sums[z, a] * found
            panel_ref[0, a] = panel
            total += dot_t(dense[row_start + a], panel)
    share[...] = total

    def d_copy(o):
        return pltpu.make_async_remote_copy(
            share,
            shares.at[o - 1],
            d_send.at[o - 1],
            d_recv.at[o - 1],
            at(z, None, lax.rem(row + o, rows)),
            MESH,
        )

    for o in range(1, rows):
        d_copy(o).start()
    diag_ref[0] -= total
    for o in range(1, rows):
        d_copy(o).wait_recv()
        diag_ref[0] -= shares[o - 1]

    for o in range(1, rows):
        d_copy(o).wait_send()
    for c in range(chunks):
        y_copy(c).wait_send()

    @pl.loop(0, planes - 1)
    def _(n):
        d = order(n)
        w_copy(d).wait_send()
        f_copy(d).wait_send()
        for c in range(chunks):
            r_copy(d, c, d, d).wait_send()


def local(sigma_anc, panel_u, structure, diag_inv):
    row_count, col_count, width = sigma_anc.shape[0], sigma_anc.shape[1], sigma_anc.shape[2]
    cols, rows = lax.axis_size("col"), lax.axis_size("row")
    planes = cols // 2
    plane_cols = 2 * col_count
    chunks = next(c for c in (4, 2, 1) if row_count % c == 0)
    block = (width, width)
    f32, bf16 = jnp.float32, jnp.bfloat16
    vmem = pl.BlockSpec(memory_space=pltpu.VMEM)
    dma = pltpu.SemaphoreType.DMA
    return pl.pallas_call(
        functools.partial(kernel, planes, rows, chunks),
        out_shape=(
            jax.ShapeDtypeStruct((1, row_count, *block), f32),
            jax.ShapeDtypeStruct((1, *block), f32),
        ),
        in_specs=[vmem, vmem, pl.BlockSpec(memory_space=pltpu.SMEM), vmem],
        out_specs=(vmem, vmem),
        scratch_shapes=[
            pltpu.VMEM((cols * col_count, *block), f32),
            pltpu.VMEM((planes, plane_cols, *block), f32),
            pltpu.VMEM((row_count, col_count, *block), f32),
            pltpu.VMEM((row_count, width, plane_cols * width), bf16),
            pltpu.VMEM((row_count, width, plane_cols * width), bf16),
            pltpu.VMEM((plane_cols * width, 2 * width), bf16),
            pltpu.VMEM((planes, row_count, *block), f32),
            pltpu.VMEM((planes + 1, row_count, *block), f32),
            pltpu.VMEM(block, f32),
            pltpu.VMEM((rows - 1, *block), f32),
            dma((chunks,)),
            dma((chunks,)),
            dma((planes,)),
            dma((planes,)),
            dma((planes,)),
            dma((planes,)),
            dma((planes, chunks)),
            dma((planes + 1, chunks)),
            dma((rows - 1,)),
            dma((rows - 1,)),
        ],
        compiler_params=pltpu.CompilerParams(
            collective_id=0, has_side_effects=True, vmem_limit_bytes=60 * 1024 * 1024
        ),
    )(sigma_anc, panel_u, structure, diag_inv)


def solution(mesh):
    placed = (
        P("row", "col", None, None),
        P("col", None, None, None),
        P("col", None),
        P("col", None, None),
    )
    return jax.shard_map(
        local,
        mesh=mesh,
        in_specs=placed,
        out_specs=(P("col", "row", None, None), P("col", None, None)),
        check_vma=False,
    )
```

time: 157 us -> 45.7 us (0.29); the launches traced: 155 us -> 45.5 us
  waiting for transfers between devices: 97.2 us -> 0 us
  Pallas kernels: 0 us -> 42.6 us
  blocking collectives: 31.1 us -> 0 us
  between operations: 14.1 us -> 0.65 us
  matrix products: 8.14 us -> 0 us
    reduce_scatter x1 -> x0, waiting for transfers between devices: 66.9 us -> none  [local(): lax.psum_scatter(jnp.einsum('abxz,bjzy->jaxy', sigma_anc, moved, precisio...]
    pallas_call x0 -> x1, Pallas kernels: none -> 42.6 us  [local(): pl.pallas_call(functools.partial(kernel, planes, rows, chunks), out_shape...]
    all_to_all x1 -> x0, blocking collectives: 31.1 us -> none  [local(): lax.all_to_all(dense, 'col', split_axis=0, concat_axis=1, tiled=True)]
    psum x1 -> x0, waiting for transfers between devices: 30.3 us -> none  [local(): update = lax.psum(share, 'row')]
    dot_general x4 -> x0, matrix products: 8.14 us -> none  [the longest x1 3.2 us: local(): jnp.einsum('abxz,bjzy->jaxy', sigma_anc, moved, precision=lax.Precision.H...]
  transfers between devices with their start and end apart: 2 -> 0, of which waited for: 2 -> 0; matrix products, arithmetic and copies ran while one was open for 1% -> 0% of each run, Pallas kernels for 0% -> 0%
where the time goes in v1:
time: 45.7 us; the launch traced here: 45.5 us
  Pallas kernels  42.6 us (93%)
  local copies, waits for them, and re-layouts  2.34 us (5%)
  between operations  0.65 us (1%)
    pallas_call x1, Pallas kernels, local(): pl.pallas_call(functools.partial(kernel, planes, rows, chunks), out_shape...  42.6 us
    unnamed x4, local copies, waits for them, and re-layouts  2.34 us

profile of v1, /device:TPU:1, one launch (start us, length us, event | category | flops | bytes accessed | tf_op | source)
XLA Modules:
  0.0 45.5 jit_solution(7091925600771984118)
XLA Ops:
  0.6 42.6 %shard_map.59 = (f32[1,4,128,128]{3,2,1,0:T(8,128)}, f32[1,128,128]{2,1,0:T(8,128)}) custom-call(f32[4,2,128,128]{3,2,1,0:T(8,128)} %sigma_ref.1, f32[1,8,128,128]{3,2,1,0:T(8,128)} %u_ref.1, s32[1,8]{1,0:T(1,128)} %s_ref.1, f32[1,128,128]{2,1,0:T(8,128)} %inv_ref.1), custom_call_target="tpu_custom_call" | custom-call | tf_op jit(solution)/shard_map/pallas_call | solution.py:296
  43.2 0.0 copy-start
  43.2 1.7 %copy.8 = f32[1,4,128,128]{3,2,1,0:T(8,128)} copy(f32[1,4,128,128]{3,2,1,0:T(8,128)} %get-tuple-element.4) | data formatting | bytes 524288
  44.9 0.0 copy-done
  44.9 0.6 %copy.9 = f32[1,128,128]{2,1,0:T(8,128)} copy(f32[1,128,128]{2,1,0:T(8,128)S(1)} %copy-done) | data formatting | bytes 131072
Async XLA Ops:
  43.2 1.7 %copy-start = (f32[1,128,128]{2,1,0:T(8,128)S(1)}, f32[1,128,128]{2,1,0:T(8,128)}, u32[]{:S(2)}) copy-start(f32[1,128,128]{2,1,0:T(8,128)} %get-tuple-element.5) | copy-start | bytes 196612

commit v2 on v1

--- a/solution.py
+++ b/solution.py
@@ -32,6 +32,8 @@
     inv_ref,
     panel_ref,
     diag_ref,
+    held,
+    u_held,
     dense,
     moved,
     other,
@@ -52,6 +54,7 @@
     r_recv,
     d_send,
     d_recv,
+    in_sem,
 ):
     row_count, col_count, width = sigma_ref.shape[0], sigma_ref.shape[1], sigma_ref.shape[2]
     plane_cols = 2 * col_count
@@ -71,6 +74,11 @@
         left_first = jnp.where(n < z, n, planes - 1 - (n - z))
         return jnp.where(2 * z < planes, right_first, left_first)
 
+    u_in = pltpu.make_async_copy(u_ref, u_held, in_sem.at[0])
+    sigma_in = pltpu.make_async_copy(sigma_ref, held, in_sem.at[1])
+    u_in.start()
+    sigma_in.start()
+
     barrier = pltpu.get_barrier_semaphore()
     pl.semaphore_signal(barrier, inc=1, device_id=at(z, 1 - y), device_id_type=MESH)
 
@@ -90,13 +98,12 @@
             found, where = jnp.where(hit, 1, found), jnp.where(hit, k, where)
         return found.astype(jnp.float32), where
 
+    u_in.wait()
+
     @pl.loop(0, dense.shape[0])
     def _(b):
         found, where = member(b)
-        dense[b] = u_ref[0, where] * found
-
-    inv = inv_ref[0]
-    diag_ref[0] = dot_t(inv, inv)
+        dense[b] = u_held[0, where] * found
 
     def plane_part(plane, part):
         lane = jnp.where(part == 0, y, 1 - y)
@@ -168,45 +175,82 @@
     def load_w(d):
         for i in range(plane_cols):
             high, low = split(moved[d, i])
-            w_cat[i * width : (i + 1) * width, :width] = high
-            w_cat[i * width : (i + 1) * width, width:] = low
+            w_cat[d, i * width : (i + 1) * width, :width] = high
+            w_cat[d, i * width : (i + 1) * width, width:] = low
 
     def convert(c):
         for q in range(step_rows):
             a = c * step_rows + q
-            for source, base in ((sigma_ref, 0), (other, col_count)):
+            for source, base in ((held, 0), (other, col_count)):
                 for i in range(col_count):
                     high, low = split(source[a, i])
                     lanes = slice((base + i) * width, (base + i + 1) * width)
                     sig_hi[a, :, lanes] = high
                     sig_lo[a, :, lanes] = low
 
-    def product(a):
-        both = jnp.dot(sig_hi[a], w_cat[...], preferred_element_type=jnp.float32)
-        low = jnp.dot(sig_lo[a], w_cat[:, :width], preferred_element_type=jnp.float32)
+    def product(a, d):
+        both = jnp.dot(sig_hi[a], w_cat[d], preferred_element_type=jnp.float32)
+        low = jnp.dot(sig_lo[a], w_cat[d, :, :width], preferred_element_type=jnp.float32)
         return both[:, :width] + (both[:, width:] + low)
 
-    forward(order(0))
-
-    @pl.loop(0, planes - 1)
-    def _(n):
-        d = order(n)
-        right = d > z
-        f_arrival(d).wait_recv()
-        load_w(d)
-        has_up = jnp.where(right, z > 0, z < planes - 1)
-        target = jnp.where(right, z + 1, z - 1)
-        slot = jnp.where(right, d, jnp.where(d == z - 1, planes, d))
-        for c in range(chunks):
-
-            @pl.when(n == 0)
-            def _():
-                y_copy(c).wait_recv()
-                convert(c)
-
+    row_start = row * row_count
+
+    def own(c):
+        for q in range(step_rows):
+            sums[z, c * step_rows + q] = product(c * step_rows + q, z)
+
+        @pl.when(z > 0)
+        def _():
+            r_arrival(z, c).wait_recv()
             for q in range(step_rows):
                 a = c * step_rows + q
-                sums[d, a] = product(a)
+                sums[z, a] += came[z, a]
+
+        @pl.when(z < planes - 1)
+        def _():
+            r_arrival(planes, c).wait_recv()
+            for q in range(step_rows):
+                a = c * step_rows + q
+                sums[z, a] += came[planes, a]
+
+        for q in range(step_rows):
+            a = c * step_rows + q
+            found, _ = member(row_start + a)
+            panel = -sums[z, a] * found
+            panel_ref[0, a] = panel
+            share[...] += dot_t(dense[row_start + a], panel)
+
+    inv = inv_ref[0]
+    diag_ref[0] = dot_t(inv, inv)
+    share[...] = jnp.zeros_like(share)
+    load_w(z)
+    sigma_in.wait()
+    forward(order(0))
+    y_copy(0).wait_recv()
+    convert(0)
+
+    @pl.loop(0, chunks)
+    def _(c):
+        @pl.loop(0, planes - 1)
+        def _(n):
+            d = order(n)
+            right = d > z
+            has_up = jnp.where(right, z > 0, z < planes - 1)
+            target = jnp.where(right, z + 1, z - 1)
+            slot = jnp.where(right, d, jnp.where(d == z - 1, planes, d))
+
+            @pl.when(c == 0)
+            def _():
+                @pl.when(n + 1 < planes - 1)
+                def _():
+                    forward(order(n + 1))
+
+                f_arrival(d).wait_recv()
+                load_w(d)
+
+            for q in range(step_rows):
+                a = c * step_rows + q
+                sums[d, a] = product(a, d)
 
             @pl.when(has_up)
             def _():
@@ -217,40 +261,17 @@
 
             r_copy(d, c, slot, target).start()
 
-            if c == chunks // 2:
-
-                @pl.when(n + 1 < planes - 1)
-                def _():
-                    forward(order(n + 1))
-
-    load_w(z)
-    for a in range(row_count):
-        sums[z, a] = product(a)
-    row_start = row * row_count
-    total = jnp.zeros((width, width), jnp.float32)
-    for c in range(chunks):
-
-        @pl.when(z > 0)
+        @pl.when(c + 1 < chunks)
         def _():
-            r_arrival(z, c).wait_recv()
-            for q in range(step_rows):
-                a = c * step_rows + q
-                sums[z, a] += came[z, a]
-
-        @pl.when(z < planes - 1)
+            y_copy(c + 1).wait_recv()
+            convert(c + 1)
+
+        @pl.when(c > 0)
         def _():
-            r_arrival(planes, c).wait_recv()
-            for q in range(step_rows):
-                a = c * step_rows + q
-                sums[z, a] += came[planes, a]
-
-        for q in range(step_rows):
-            a = c * step_rows + q
-            found, _ = member(row_start + a)
-            panel = -sums[z, a] * found
-            panel_ref[0, a] = panel
-            total += dot_t(dense[row_start + a], panel)
-    share[...] = total
+            own(c - 1)
+
+    own(chunks - 1)
+    total = share[...]
 
     def d_copy(o):
         return pltpu.make_async_remote_copy(
@@ -292,6 +313,7 @@
     block = (width, width)
     f32, bf16 = jnp.float32, jnp.bfloat16
     vmem = pl.BlockSpec(memory_space=pltpu.VMEM)
+    hbm = pl.BlockSpec(memory_space=pl.ANY)
     dma = pltpu.SemaphoreType.DMA
     return pl.pallas_call(
         functools.partial(kernel, planes, rows, chunks),
@@ -299,15 +321,17 @@
             jax.ShapeDtypeStruct((1, row_count, *block), f32),
             jax.ShapeDtypeStruct((1, *block), f32),
         ),
-        in_specs=[vmem, vmem, pl.BlockSpec(memory_space=pltpu.SMEM), vmem],
+        in_specs=[hbm, hbm, pl.BlockSpec(memory_space=pltpu.SMEM), vmem],
         out_specs=(vmem, vmem),
         scratch_shapes=[
+            pltpu.VMEM(sigma_anc.shape, f32),
+            pltpu.VMEM(panel_u.shape, f32),
             pltpu.VMEM((cols * col_count, *block), f32),
             pltpu.VMEM((planes, plane_cols, *block), f32),
             pltpu.VMEM((row_count, col_count, *block), f32),
             pltpu.VMEM((row_count, width, plane_cols * width), bf16),
             pltpu.VMEM((row_count, width, plane_cols * width), bf16),
-            pltpu.VMEM((plane_cols * width, 2 * width), bf16),
+            pltpu.VMEM((planes, plane_cols * width, 2 * width), bf16),
             pltpu.VMEM((planes, row_count, *block), f32),
             pltpu.VMEM((planes + 1, row_count, *block), f32),
             pltpu.VMEM(block, f32),
@@ -322,6 +346,7 @@
             dma((planes + 1, chunks)),
             dma((rows - 1,)),
             dma((rows - 1,)),
+            dma((2,)),
         ],
         compiler_params=pltpu.CompilerParams(
             collective_id=0, has_side_effects=True, vmem_limit_bytes=60 * 1024 * 1024

time: 45.7 us -> 50.1 us (1.096)
  Pallas kernels: 42.6 us -> 46.9 us
    pallas_call x1, Pallas kernels: 42.6 us -> 46.9 us  [local(): pl.pallas_call(functools.partial(kernel, planes, rows, chunks), out_shape...]
where the time goes in v2:
time: 50.1 us; the launch traced here: 49.9 us
  Pallas kernels  46.9 us (94%)
  local copies, waits for them, and re-layouts  2.34 us (5%)
  between operations  0.65 us (1%)
    pallas_call x1, Pallas kernels, local(): pl.pallas_call(functools.partial(kernel, planes, rows, chunks), out_shape...  46.9 us
    unnamed x4, local copies, waits for them, and re-layouts  2.34 us

profile of v2, /device:TPU:1, one launch (start us, length us, event | category | flops | bytes accessed | tf_op | source)
XLA Modules:
  0.0 49.9 jit_solution(4678593621026534746)
XLA Ops:
  0.6 46.9 %shard_map.59 = (f32[1,4,128,128]{3,2,1,0:T(8,128)}, f32[1,128,128]{2,1,0:T(8,128)}) custom-call(f32[4,2,128,128]{3,2,1,0:T(8,128)} %sigma_ref.1, f32[1,8,128,128]{3,2,1,0:T(8,128)} %u_ref.1, s32[1,8]{1,0:T(1,128)} %s_ref.1, f32[1,128,128]{2,1,0:T(8,128)} %inv_ref.1), custom_call_target="tpu_custom_call" | custom-call | tf_op jit(solution)/shard_map/pallas_call | solution.py:318
  47.5 0.0 copy-start
  47.5 1.7 %copy.8 = f32[1,4,128,128]{3,2,1,0:T(8,128)} copy(f32[1,4,128,128]{3,2,1,0:T(8,128)} %get-tuple-element.4) | data formatting | bytes 524288
  49.2 0.0 copy-done
  49.2 0.6 %copy.9 = f32[1,128,128]{2,1,0:T(8,128)} copy(f32[1,128,128]{2,1,0:T(8,128)S(1)} %copy-done) | data formatting | bytes 131072
Async XLA Ops:
  47.5 1.7 %copy-start = (f32[1,128,128]{2,1,0:T(8,128)S(1)}, f32[1,128,128]{2,1,0:T(8,128)}, u32[]{:S(2)}) copy-start(f32[1,128,128]{2,1,0:T(8,128)} %get-tuple-element.5) | copy-start | bytes 196612

commit v3 on v1

--- a/solution.py
+++ b/solution.py
@@ -217,7 +217,7 @@
 
             r_copy(d, c, slot, target).start()
 
-            if c == chunks // 2:
+            if c == 0:
 
                 @pl.when(n + 1 < planes - 1)
                 def _():

time: 45.7 us -> 43.8 us (0.958)
  Pallas kernels: 42.6 us -> 40.6 us
    pallas_call x1, Pallas kernels: 42.6 us -> 40.6 us  [local(): pl.pallas_call(functools.partial(kernel, planes, rows, chunks), out_shape...]
where the time goes in v3:
time: 43.8 us; the launch traced here: 43.6 us
  Pallas kernels  40.6 us (93%)
  local copies, waits for them, and re-layouts  2.34 us (5%)
  between operations  0.65 us (1%)
    pallas_call x1, Pallas kernels, local(): pl.pallas_call(functools.partial(kernel, planes, rows, chunks), out_shape...  40.6 us
    unnamed x4, local copies, waits for them, and re-layouts  2.34 us

profile of v3, /device:TPU:1, one launch (start us, length us, event | category | flops | bytes accessed | tf_op | source)
XLA Modules:
  0.0 43.6 jit_solution(4327222706440209106)
XLA Ops:
  0.6 40.6 %shard_map.59 = (f32[1,4,128,128]{3,2,1,0:T(8,128)}, f32[1,128,128]{2,1,0:T(8,128)}) custom-call(f32[4,2,128,128]{3,2,1,0:T(8,128)} %sigma_ref.1, f32[1,8,128,128]{3,2,1,0:T(8,128)} %u_ref.1, s32[1,8]{1,0:T(1,128)} %s_ref.1, f32[1,128,128]{2,1,0:T(8,128)} %inv_ref.1), custom_call_target="tpu_custom_call" | custom-call | tf_op jit(solution)/shard_map/pallas_call | solution.py:296
  41.3 0.0 copy-start
  41.3 1.7 %copy.8 = f32[1,4,128,128]{3,2,1,0:T(8,128)} copy(f32[1,4,128,128]{3,2,1,0:T(8,128)} %get-tuple-element.4) | data formatting | bytes 524288
  43.0 0.0 copy-done
  43.0 0.6 %copy.9 = f32[1,128,128]{2,1,0:T(8,128)} copy(f32[1,128,128]{2,1,0:T(8,128)S(1)} %copy-done) | data formatting | bytes 131072
Async XLA Ops:
  41.3 1.7 %copy-start = (f32[1,128,128]{2,1,0:T(8,128)S(1)}, f32[1,128,128]{2,1,0:T(8,128)}, u32[]{:S(2)}) copy-start(f32[1,128,128]{2,1,0:T(8,128)} %get-tuple-element.5) | copy-start | bytes 196612

commit v4 on v3

--- a/solution.py
+++ b/solution.py
@@ -142,16 +142,26 @@
             theirs, theirs, f_send.at[source], f_recv.at[source], at(z, None, mate), MESH
         )
 
-    def r_copy(d, c, slot, target):
-        rng = pl.ds(c * step_rows, step_rows)
-        return pltpu.make_async_remote_copy(
-            sums.at[d, rng], came.at[slot, rng], r_send.at[d, c], r_recv.at[slot, c], at(target), MESH
-        )
-
-    def r_arrival(slot, c):
-        rng = pl.ds(c * step_rows, step_rows)
-        return pltpu.make_async_remote_copy(
-            came.at[slot, rng], came.at[slot, rng], r_send.at[0, c], r_recv.at[slot, c], at(z, 1 - y), MESH
+    def r_copy(d, c, h, slot, target):
+        rng, lines = pl.ds(c * step_rows, step_rows), pl.ds(h * (width // 2), width // 2)
+        return pltpu.make_async_remote_copy(
+            sums.at[d, rng, lines],
+            came.at[slot, rng, lines],
+            r_send.at[d, 2 * c + h],
+            r_recv.at[slot, 2 * c + h],
+            at(target),
+            MESH,
+        )
+
+    def r_arrival(slot, c, h):
+        rng, lines = pl.ds(c * step_rows, step_rows), pl.ds(h * (width // 2), width // 2)
+        return pltpu.make_async_remote_copy(
+            came.at[slot, rng, lines],
+            came.at[slot, rng, lines],
+            r_send.at[0, 2 * c + h],
+            r_recv.at[slot, 2 * c + h],
+            at(z, 1 - y),
+            MESH,
         )
 
     for c in range(chunks):
@@ -208,14 +218,17 @@
                 a = c * step_rows + q
                 sums[d, a] = product(a)
 
-            @pl.when(has_up)
-            def _():
-                r_arrival(d, c).wait_recv()
-                for q in range(step_rows):
-                    a = c * step_rows + q
-                    sums[d, a] += came[d, a]
-
-            r_copy(d, c, slot, target).start()
+            for h in range(2):
+                lines = slice(h * (width // 2), (h + 1) * (width // 2))
+
+                @pl.when(has_up)
+                def _():
+                    r_arrival(d, c, h).wait_recv()
+                    for q in range(step_rows):
+                        a = c * step_rows + q
+                        sums[d, a, lines] += came[d, a, lines]
+
+                r_copy(d, c, h, slot, target).start()
 
             if c == 0:
 
@@ -232,14 +245,16 @@
 
         @pl.when(z > 0)
         def _():
-            r_arrival(z, c).wait_recv()
+            r_arrival(z, c, 0).wait_recv()
+            r_arrival(z, c, 1).wait_recv()
             for q in range(step_rows):
                 a = c * step_rows + q
                 sums[z, a] += came[z, a]
 
         @pl.when(z < planes - 1)
         def _():
-            r_arrival(planes, c).wait_recv()
+            r_arrival(planes, c, 0).wait_recv()
+            r_arrival(planes, c, 1).wait_recv()
             for q in range(step_rows):
                 a = c * step_rows + q
                 sums[z, a] += came[planes, a]
@@ -280,7 +295,8 @@
         w_copy(d).wait_send()
         f_copy(d).wait_send()
         for c in range(chunks):
-            r_copy(d, c, d, d).wait_send()
+            for h in range(2):
+                r_copy(d, c, h, d, d).wait_send()
 
 
 def local(sigma_anc, panel_u, structure, diag_inv):
@@ -318,8 +334,8 @@
             dma((planes,)),
             dma((planes,)),
             dma((planes,)),
-            dma((planes, chunks)),
-            dma((planes + 1, chunks)),
+            dma((planes, 2 * chunks)),
+            dma((planes + 1, 2 * chunks)),
             dma((rows - 1,)),
             dma((rows - 1,)),
         ],

time: 43.8 us -> 44.1 us (level)
  no operation moved by 1% of the time
where the time goes in v4:
time: 44.1 us; the launch traced here: 43.9 us
  Pallas kernels  41 us (93%)
  local copies, waits for them, and re-layouts  2.34 us (5%)
  between operations  0.65 us (1%)
    pallas_call x1, Pallas kernels, local(): pl.pallas_call(functools.partial(kernel, planes, rows, chunks), out_shape...  41 us
    unnamed x4, local copies, waits for them, and re-layouts  2.34 us

profile of v4, /device:TPU:1, one launch (start us, length us, event | category | flops | bytes accessed | tf_op | source)
XLA Modules:
  0.0 43.9 jit_solution(2670564117954330523)
XLA Ops:
  0.6 41.0 %shard_map.59 = (f32[1,4,128,128]{3,2,1,0:T(8,128)}, f32[1,128,128]{2,1,0:T(8,128)}) custom-call(f32[4,2,128,128]{3,2,1,0:T(8,128)} %sigma_ref.1, f32[1,8,128,128]{3,2,1,0:T(8,128)} %u_ref.1, s32[1,8]{1,0:T(1,128)} %s_ref.1, f32[1,128,128]{2,1,0:T(8,128)} %inv_ref.1), custom_call_target="tpu_custom_call" | custom-call | tf_op jit(solution)/shard_map/pallas_call | solution.py:312
  41.6 0.0 copy-start
  41.6 1.7 %copy.8 = f32[1,4,128,128]{3,2,1,0:T(8,128)} copy(f32[1,4,128,128]{3,2,1,0:T(8,128)} %get-tuple-element.4) | data formatting | bytes 524288
  43.3 0.0 copy-done
  43.3 0.6 %copy.9 = f32[1,128,128]{2,1,0:T(8,128)} copy(f32[1,128,128]{2,1,0:T(8,128)S(1)} %copy-done) | data formatting | bytes 131072
Async XLA Ops:
  41.6 1.7 %copy-start = (f32[1,128,128]{2,1,0:T(8,128)S(1)}, f32[1,128,128]{2,1,0:T(8,128)}, u32[]{:S(2)}) copy-start(f32[1,128,128]{2,1,0:T(8,128)} %get-tuple-element.5) | copy-start | bytes 196612
